TPU v7x, 32 devices: a whole 2x2x4 slice. The times are simulated.
32 devices in a mesh: seq: 8 (over y, x, core), wshard: 4 (over z).
Axes of the slice: x: 2, y: 2, z: 4, core: 2. Of those that a mesh axis runs over, the one named last changes fastest.
Arguments:
- tokens: float32 [6144, 768], P(('seq', 'wshard')), may hold values from -18 to 18, as said below
- attention_norm_gain: float32 [2, 768], replicated, may hold values from 0.5 to 1.5
- qkv_weight: bfloat16 [2, 768, 2304], P(None, None, 'wshard'), may hold values from -7 to 7, as said below
- output_weight: bfloat16 [2, 768, 768], P(None, None, 'wshard'), may hold values from -0.75 to 0.75
- feedforward_norm_gain: float32 [2, 768], replicated, may hold values from 0.5 to 1.5
- input_weight: bfloat16 [2, 768, 2304], P(None, None, 'wshard'), may hold values from -0.21875 to 0.21875
- down_weight: bfloat16 [2, 1152, 768], P(None, 'wshard'), may hold values from -0.1875 to 0.1875
- cotangent: float32 [6144, 768], P(('seq', 'wshard')), may hold values from -18 to 18
Outputs:
- outputs: float32 [6144, 768], P(('seq', 'wshard'))
- input_grad: float32 [6144, 768], P(('seq', 'wshard'))
- grad_attention_gain: float32 [2, 768], replicated
- grad_qkv_weight: float32 [2, 768, 2304], P(None, 'seq', 'wshard')
- grad_output_weight: float32 [2, 768, 768], P(None, 'seq', 'wshard')
- grad_feedforward_gain: float32 [2, 768], replicated
- grad_input_weight: float32 [2, 768, 2304], P(None, 'seq', 'wshard')
- grad_down_weight: float32 [2, 1152, 768], P(None, 'wshard', 'seq')
Inputs may be any that keep to these rules, and one draw needn't show every extreme that they name: `tokens`: activations of the first layer. `qkv_weight`: columns hold queries, keys, values, each head by head.
All inputs are finite; a program needn't handle non-finite values.
Results may differ from a plain program's by a relative error of at most 0.022.
Values may be sent and summed in bfloat16 or wider, within the bound.
A program may use at most 192 MiB of HBM per device.

v0:
```python
import math

import jax
import jax.numpy as jnp
from jax import lax
from jax.experimental import pallas as pl
from jax.experimental.pallas import tpu as pltpu
from jax.sharding import PartitionSpec as P

D = 768
HEADS = 12
HDIM = 64
FF = 1152
WIN = 64
LAYERS = 2
SEQS = 1


EPSILON = 1e-05
THETA = 10000.0


def with_halo(cells, sides, width):
    for axis, dim in sides:
        count = lax.axis_size(axis)
        ends = count - 1
        head = lax.slice_in_dim(cells, 0, width, axis=dim)
        tail = lax.slice_in_dim(cells, cells.shape[dim] - width, cells.shape[dim], axis=dim)
        cells = jnp.concatenate(
            [
                lax.ppermute(tail, axis, [(i, (i + 1) % count) for i in range(ends)]),
                cells,
                lax.ppermute(head, axis, [((i + 1) % count, i) for i in range(ends)]),
            ],
            axis=dim,
        )
    return cells


def rope_tables(positions):
    middle_state = HDIM // 2
    inverse = THETA ** (-(jnp.arange(middle_state, dtype=jnp.float32) * (2.0 / HDIM)))
    angles = positions.astype(jnp.float32)[:, None] * inverse[None, :]
    return (
        jnp.concatenate([jnp.cos(angles)] * 4, axis=1),
        jnp.concatenate([jnp.sin(angles)] * 4, axis=1),
    )


def layer_normalize(hidden_state):
    centred = hidden_state - jnp.mean(hidden_state, axis=-1, keepdims=True)
    inverse = lax.rsqrt(jnp.mean(centred * centred, axis=-1, keepdims=True) + EPSILON)
    return (centred * inverse, inverse)


def norm_backward_step(normalized_gradient, normed, inverse, gain_row):
    scaled = normalized_gradient * gain_row
    result = (
        scaled
        - jnp.mean(scaled, axis=-1, keepdims=True)
        - normed * jnp.mean(scaled * normed, axis=-1, keepdims=True)
    )
    return (result * inverse, jnp.sum(normalized_gradient * normed, axis=0))


def gelu_exact(inner_activation):
    return 0.5 * inner_activation * (1.0 + lax.erf(inner_activation * (1.0 / math.sqrt(2.0))))


def gelu_slope(inner_activation):
    return 0.5 * (
        1.0 + lax.erf(inner_activation * (1.0 / math.sqrt(2.0)))
    ) + inner_activation * jnp.exp(-0.5 * inner_activation * inner_activation) * (
        1.0 / math.sqrt(2.0 * math.pi)
    )


def lane_half(shape):
    return lax.rem(lax.broadcasted_iota(jnp.int32, shape, 1), HDIM) < HDIM // 2


def rotate_lanes(values, sign):
    width = values.shape[1]
    ahead = pltpu.roll(values, width - HDIM // 2, 1)
    behind = pltpu.roll(values, HDIM // 2, 1)
    return jnp.where(lane_half(values.shape), -sign * ahead, sign * behind)


def spread(table):
    return jnp.concatenate([table] * (D // table.shape[1]), axis=1)


def rope_kernel(qkv_ref, cosine_ref, sine_ref, query_ref, kv_ref):
    cosine = spread(cosine_ref[...])
    sine = spread(sine_ref[...])
    queries = qkv_ref[:, :D]
    keys = qkv_ref[:, D : 2 * D]
    query_ref[...] = (queries * cosine + rotate_lanes(queries, 1.0) * sine).astype(jnp.bfloat16)
    kv_ref[:, :D] = (keys * cosine + rotate_lanes(keys, 1.0) * sine).astype(jnp.bfloat16)
    kv_ref[:, D:] = qkv_ref[:, 2 * D :].astype(jnp.bfloat16)


def dot_f32(left, right, dims):
    return lax.dot_general(left, right, (dims, ((), ())), preferred_element_type=jnp.float32)


def head_scores(queries, keys, allowed):
    scores = dot_f32(queries, keys, ((1,), (1,))) * (1.0 / math.sqrt(HDIM))
    return jnp.where(allowed, scores, -1e30)


def window_mask(bounds_ref, rows):
    shape = (rows, rows + 2 * WIN)
    query = lax.broadcasted_iota(jnp.int32, shape, 0)
    key = lax.broadcasted_iota(jnp.int32, shape, 1)
    near = (key >= query) & (key <= query + 2 * WIN)
    return near & (key >= bounds_ref[0]) & (key < bounds_ref[1])


def forward_kernel(bounds_ref, query_ref, kv_ref, context_ref, log_ref):
    rows = query_ref.shape[0]
    allowed = window_mask(bounds_ref, rows)
    logs = []
    for head in range(HEADS):
        cols = slice(head * HDIM, (head + 1) * HDIM)
        shifted = slice(D + head * HDIM, D + (head + 1) * HDIM)
        scores = head_scores(query_ref[:, cols], kv_ref[:, cols], allowed)
        top = jnp.max(scores, axis=1, keepdims=True)
        log_total = top + jnp.log(jnp.sum(jnp.exp(scores - top), axis=1, keepdims=True))
        probs = jnp.exp(scores - log_total).astype(jnp.bfloat16)
        context_ref[:, cols] = dot_f32(probs, kv_ref[:, shifted], ((1,), (0,))).astype(
            jnp.bfloat16
        )
        logs.append(log_total)
    log_ref[...] = jnp.concatenate(logs, axis=1)


def backward_kernel(
    bounds_ref, query_ref, kv_ref, log_ref, grad_ref, dquery_ref, local_ref, rim_ref
):
    rows = query_ref.shape[0]
    allowed = window_mask(bounds_ref, rows)
    for head in range(HEADS):
        cols = slice(head * HDIM, (head + 1) * HDIM)
        shifted = slice(D + head * HDIM, D + (head + 1) * HDIM)
        queries = query_ref[:, cols]
        keys = kv_ref[:, cols]
        grads = grad_ref[:, cols]
        scores = head_scores(queries, keys, allowed)
        probs = jnp.exp(scores - log_ref[:, head : head + 1])
        grad_values = dot_f32(probs.astype(jnp.bfloat16), grads, ((0,), (0,)))
        grad_probs = dot_f32(grads, kv_ref[:, shifted], ((1,), (1,)))
        inner = jnp.sum(probs * grad_probs, axis=1, keepdims=True)
        grad_scores = (probs * (grad_probs - inner) * (1.0 / math.sqrt(HDIM))).astype(jnp.bfloat16)
        dquery_ref[:, cols] = dot_f32(grad_scores, keys, ((1,), (0,)))
        grad_keys = dot_f32(grad_scores, queries, ((0,), (0,)))
        for place, value in ((cols, grad_keys), (shifted, grad_values)):
            local_ref[:, place] = value[WIN : WIN + rows]
            rim_ref[:WIN, place] = value[:WIN].astype(jnp.bfloat16)
            rim_ref[WIN:, place] = value[WIN + rows :].astype(jnp.bfloat16)


def unrope_kernel(dquery_ref, local_ref, low_ref, high_ref, cosine_ref, sine_ref, out_ref):
    rows = dquery_ref.shape[0]
    cosine = spread(cosine_ref[...])
    sine = spread(sine_ref[...])
    queries = dquery_ref[...]
    out_ref[:, :D] = (queries * cosine - rotate_lanes(queries * sine, 1.0)).astype(jnp.bfloat16)
    local = local_ref[...]
    top = jnp.concatenate([low_ref[...].astype(jnp.float32), jnp.zeros((rows - WIN, 2 * D), jnp.float32)], axis=0)
    bottom = jnp.concatenate([jnp.zeros((rows - WIN, 2 * D), jnp.float32), high_ref[...].astype(jnp.float32)], axis=0)
    local = local + top + bottom
    keys = local[:, :D]
    out_ref[:, D : 2 * D] = (keys * cosine - rotate_lanes(keys * sine, 1.0)).astype(jnp.bfloat16)
    out_ref[:, 2 * D :] = local[:, D:].astype(jnp.bfloat16)


def local_call(kernel, outs, flops, operands, scalars=False):
    moved = sum(x.size * x.dtype.itemsize for x in operands) + sum(
        math.prod(shape) * jnp.dtype(kind).itemsize for shape, kind in outs
    )
    specs = [pl.BlockSpec(memory_space=pltpu.VMEM)] * len(operands)
    if scalars:
        specs[0] = pl.BlockSpec(memory_space=pltpu.SMEM)
    return pl.pallas_call(
        kernel,
        out_shape=[jax.ShapeDtypeStruct(shape, kind) for shape, kind in outs],
        in_specs=specs,
        out_specs=[pl.BlockSpec(memory_space=pltpu.VMEM)] * len(outs),
        cost_estimate=pl.CostEstimate(flops=flops, bytes_accessed=moved, transcendentals=0),
        compiler_params=pltpu.CompilerParams(vmem_limit_bytes=40 * 1024 * 1024),
    )(*operands)


def gather_all(share, n_w, n_seq):
    whole = lax.all_gather(share, ("wshard", "seq"), axis=0, tiled=False)
    return whole.reshape(n_w, n_seq * share.shape[0], share.shape[1])


def sum_over_blocks(terms, n_w, n_seq):
    depth = terms.shape[1] // n_seq
    parts = terms.reshape(n_w, n_seq, depth, terms.shape[2]).transpose(1, 0, 2, 3)
    parts = parts.reshape(n_seq * n_w, depth, terms.shape[2])
    return lax.psum_scatter(parts, "seq", scatter_dimension=0, tiled=True)


def sum_everywhere(values, axes):
    for axis in axes:
        count = lax.axis_size(axis)
        if count & (count - 1):
            values = lax.psum(values, axis)
            continue
        step = 1
        while step < count:
            pairs = [(i, i ^ step) for i in range(count)]
            values = values + lax.ppermute(values, axis, pairs)
            step *= 2
    return values


def per_device(
    tokens,
    attention_norm_gain,
    qkv_weight,
    output_weight,
    feedforward_norm_gain,
    input_weight,
    down_weight,
    cotangent,
):
    rows = tokens.shape[0]
    total_tokens = rows * lax.axis_size("seq") * lax.axis_size("wshard")
    length = total_tokens // SEQS
    block_index = lax.axis_index("seq") * lax.axis_size("wshard") + lax.axis_index("wshard")
    query_pos = block_index * rows + jnp.arange(rows, dtype=jnp.int32)
    begin = block_index * rows - WIN
    first = begin + WIN - (begin + WIN) % length
    bounds = jnp.stack([first - begin, first + length - begin]).astype(jnp.int32)
    cosine, sine = rope_tables(query_pos % length)
    scale_grad = 1.0 / math.sqrt(total_tokens)
    n_seq = lax.axis_size("seq")
    n_w = lax.axis_size("wshard")
    strip = D // n_seq
    seq_index = lax.axis_index("seq")
    col_qkv = qkv_weight.shape[2]
    col_out = output_weight.shape[2]
    col_in = input_weight.shape[2]
    row_down = down_weight.shape[1]

    def own_strip(weight, axis):
        return lax.dynamic_slice_in_dim(weight, seq_index * strip, strip, axis)

    gathered = []
    for layer_number in range(LAYERS):
        share = jnp.concatenate(
            [
                own_strip(qkv_weight[layer_number], 0),
                own_strip(input_weight[layer_number], 0),
                own_strip(down_weight[layer_number], 1).T,
                own_strip(output_weight[layer_number], 0),
            ],
            axis=1,
        )
        whole = gather_all(share, n_w, n_seq)
        ends = (col_qkv, col_qkv + col_in, col_qkv + col_in + row_down)
        gathered.append(
            (
                whole[:, :, : ends[0]],
                whole[:, :, ends[0] : ends[1]],
                whole[:, :, ends[1] : ends[2]],
                whole[:, :, ends[2] :],
            )
        )

    def columns_product(left, weight):
        return jnp.concatenate(
            [jnp.dot(left, weight[i], preferred_element_type=jnp.float32) for i in range(n_w)],
            axis=1,
        )

    def rows_product(left, weight):
        return jnp.einsum(
            "twf,wdf->td",
            left.reshape(rows, n_w, weight.shape[2]),
            weight,
            preferred_element_type=jnp.float32,
        )

    def blocks(left, right, width):
        return (
            jnp.einsum(
                "td,twf->wdf",
                left,
                right.reshape(rows, n_w, width),
                preferred_element_type=jnp.float32,
            )
            * scale_grad
        ).astype(jnp.bfloat16)

    hidden_state = tokens
    saved_activations = []
    for layer_number in range(LAYERS):
        full_qkv, full_in, full_down, full_out = gathered[layer_number]
        attention_standardized, attention_inverse_deviation = layer_normalize(hidden_state)
        attention_normalized = (attention_standardized * attention_norm_gain[layer_number]).astype(
            jnp.bfloat16
        )
        qkv = columns_product(attention_normalized, full_qkv)
        query_matrix, kv_rows = local_call(
            rope_kernel,
            [((rows, D), jnp.bfloat16), ((rows, 2 * D), jnp.bfloat16)],
            8 * rows * D,
            (qkv, cosine, sine),
        )
        padded = with_halo(kv_rows, ((("seq", "wshard"), 0),), WIN)
        context_rows, log_total = local_call(
            forward_kernel,
            [((rows, D), jnp.bfloat16), ((rows, HEADS), jnp.float32)],
            4 * rows * padded.shape[0] * D,
            (bounds, query_matrix, padded),
            True,
        )
        middle_state = hidden_state + columns_product(context_rows, full_out)
        feedforward_standardized, feedforward_inverse_deviation = layer_normalize(middle_state)
        feedforward_normalized = (
            feedforward_standardized * feedforward_norm_gain[layer_number]
        ).astype(jnp.bfloat16)
        inner_activation = columns_product(feedforward_normalized, full_in)
        gated_linear_output = (
            gelu_exact(inner_activation[:, :FF]) * inner_activation[:, FF:]
        ).astype(jnp.bfloat16)
        holding = None
        saved_activations.append(
            (
                holding,
                attention_standardized,
                attention_inverse_deviation,
                attention_normalized,
                query_matrix,
                padded,
                log_total,
                context_rows,
                feedforward_standardized,
                feedforward_inverse_deviation,
                feedforward_normalized,
                inner_activation,
                gated_linear_output,
            )
        )
        hidden_state = middle_state + rows_product(gated_linear_output, full_down)
    grad = cotangent
    list_again, list_fgain, block_sums = ([], [], [])
    for layer_number in reversed(range(LAYERS)):
        (
            holding,
            attention_standardized,
            attention_inverse_deviation,
            attention_normalized,
            query_matrix,
            padded,
            log_total,
            context_rows,
            feedforward_standardized,
            feedforward_inverse_deviation,
            feedforward_normalized,
            inner_activation,
            gated_linear_output,
        ) = saved_activations[layer_number]
        full_qkv, full_in, full_down, full_out = gathered[layer_number]
        grad_rounded = grad.astype(jnp.bfloat16)
        local_down = blocks(grad_rounded, gated_linear_output, row_down)
        grad_geglu = columns_product(grad_rounded, full_down)
        gate = inner_activation[:, :FF]
        upper = inner_activation[:, FF:]
        grad_inner = jnp.concatenate(
            [grad_geglu * upper * gelu_slope(gate), grad_geglu * gelu_exact(gate)], axis=1
        ).astype(jnp.bfloat16)
        local_in = blocks(feedforward_normalized, grad_inner, col_in)
        feed_terms = [local_in, local_down]
        if layer_number == 0:
            block_sums.append(
                sum_over_blocks(jnp.concatenate(feed_terms, axis=2), n_w, n_seq)
            )
            feed_terms = []
        normalized_gradient = rows_product(grad_inner, full_in)
        partial_gradient, feedforward_gain_gradient = norm_backward_step(
            normalized_gradient,
            feedforward_standardized,
            feedforward_inverse_deviation,
            feedforward_norm_gain[layer_number],
        )
        list_fgain.append(feedforward_gain_gradient * scale_grad)
        grad_middle = grad + partial_gradient
        grad_middle_rounded = grad_middle.astype(jnp.bfloat16)
        local_out = blocks(context_rows, grad_middle_rounded, col_out)
        grad_context = (
            rows_product(grad_middle_rounded, full_out).astype(jnp.bfloat16)
        )
        grad_queries, local_terms, rims = local_call(
            backward_kernel,
            [
                ((rows, D), jnp.float32),
                ((rows, 2 * D), jnp.float32),
                ((2 * WIN, 2 * D), jnp.bfloat16),
            ],
            10 * rows * padded.shape[0] * D,
            (bounds, query_matrix, padded, log_total, grad_context),
            True,
        )
        sites = ("seq", "wshard")
        count = lax.axis_size(sites)
        low = lax.ppermute(rims[WIN:], sites, [(i, i + 1) for i in range(count - 1)])
        high = lax.ppermute(rims[:WIN], sites, [(i + 1, i) for i in range(count - 1)])
        (grad_qkv,) = local_call(
            unrope_kernel,
            [((rows, 3 * D), jnp.bfloat16)],
            12 * rows * D,
            (grad_queries, local_terms, low, high, cosine, sine),
        )
        local_qkv = blocks(attention_normalized, grad_qkv, col_qkv)
        block_sums.append(
            sum_over_blocks(
                jnp.concatenate(feed_terms + [local_qkv, local_out], axis=2), n_w, n_seq
            )
        )
        attention_normalized_gradient = rows_product(grad_qkv, full_qkv)
        attention_partial_gradient, attention_gain_gradient = norm_backward_step(
            attention_normalized_gradient,
            attention_standardized,
            attention_inverse_deviation,
            attention_norm_gain[layer_number],
        )
        list_again.append(attention_gain_gradient * scale_grad)
        grad = grad_middle + attention_partial_gradient
    gain_sums = sum_everywhere(
        jnp.concatenate([jnp.stack(list_again[::-1]), jnp.stack(list_fgain[::-1])], axis=0),
        ("seq", "wshard"),
    )
    summed = lax.psum_scatter(
        jnp.concatenate(block_sums, axis=2), "wshard", scatter_dimension=0, tiled=True
    )[0].astype(jnp.float32)
    per_layer = (col_in, row_down, col_qkv, col_out)
    pieces = []
    start = 0
    for width in per_layer * LAYERS:
        pieces.append(summed[:, start : start + width])
        start += width
    by_kind = [
        jnp.stack([pieces[4 * (LAYERS - 1 - n) + kind] for n in range(LAYERS)]) for kind in range(4)
    ]
    return (
        hidden_state,
        grad,
        gain_sums[:LAYERS],
        by_kind[2],
        by_kind[3],
        gain_sums[LAYERS:],
        by_kind[0],
        jnp.swapaxes(by_kind[1], 1, 2),
    )


def solution(mesh):
    placed = (
        P(("seq", "wshard"), None),
        P(),
        P(None, None, "wshard"),
        P(None, None, "wshard"),
        P(),
        P(None, None, "wshard"),
        P(None, "wshard", None),
        P(("seq", "wshard"), None),
    )
    return jax.shard_map(
        per_device,
        mesh=mesh,
        in_specs=placed,
        out_specs=(
            P(("seq", "wshard"), None),
            P(("seq", "wshard"), None),
            P(),
            P(None, "seq", "wshard"),
            P(None, "seq", "wshard"),
            P(),
            P(None, "seq", "wshard"),
            P(None, "wshard", "seq"),
        ),
        check_vma=False,
    )
```

profile of v0, /device:TPU:0, one launch (start us, length us, event | category | flops | bytes accessed | tf_op | source)
XLA Modules:
  0.0 673.1 jit_solution(474436182724819620)
XLA Ops:
  19.3 84.2 %all-gather.5.cloned.1.call-done = bf16[3072,1632]{1,0:T(8,128)(2,1)} async-done(((bf16[96,1632]{1,0:T(8,128)(2,1)}), bf16[3072,1632]{1,0:T(8,128)(2,1)}) %all-gather.5.cloned.1.call-update) | async-done | bytes 10027024 | tf_op jit(solution)/shard_map/all_gather | solution.py:196
  113.1 76.9 %all-gather.7.cloned.1.call-done = bf16[3072,1632]{1,0:T(8,128)(2,1)} async-done(((bf16[96,1632]{1,0:T(8,128)(2,1)}), bf16[3072,1632]{1,0:T(8,128)(2,1)}) %all-gather.7.cloned.1.call-update) | async-done | bytes 10027024 | tf_op jit(solution)/shard_map/all_gather | solution.py:196
  204.8 7.7 %collective-permute-done.1 = bf16[64,1536]{1,0:T(8,128)(2,1)S(1)} collective-permute-done((bf16[64,1536]{1,0:T(8,128)(2,1)S(1)}, bf16[64,1536]{1,0:T(8,128)(2,1)S(1)}, u32[]{:S(2)}, u32[]{:S(2)}) %collective-permute-start.1) | collective-permute-done | bytes 196640 | tf_op jit(solution)/shard_map/ppermute | solution.py:33
  212.5 5.8 shard_map.144
  268.2 6.6 collective-permute-done.3
  274.9 5.8 shard_map.146
  297.0 5.3 multiply_reduce_fusion
  307.3 6.6 shard_map.147
  319.8 9.3 %collective-permute-done.5.high_ref = bf16[64,1536]{1,0:T(8,128)(2,1)S(1)} collective-permute-done((bf16[64,1536]{1,0:T(8,128)(2,1)S(1)}, bf16[64,1536]{1,0:T(8,128)(2,1)S(1)}, u32[]{:S(2)}, u32[]{:S(2)}) %collective-permute-start.5) | collective-permute-done | bytes 196640 | tf_op jit(solution)/shard_map/ppermute | solution.py:413
  332.1 4.7 multiply_reduce_fusion.2
  354.4 4.9 multiply_reduce_fusion.1
  364.0 6.9 %shard_map.149 = (f32[192,768]{1,0:T(8,128)S(1)}, f32[192,1536]{1,0:T(8,128)S(1)}, bf16[128,1536]{1,0:T(8,128)(2,1)S(1)}) custom-call(s32[2]{0:T(128)S(1)} %pad_add_fusion.bounds_ref, bf16[192,768]{1,0:T(8,128)(2,1)S(1)} %get-tuple-element.22.query_ref, bf16[320,1536]{1,0:T(8,128)(2,1)S(1)} %copy-done.1, f32[192,12]{1,0:T(8,128)S(1)} %get-tuple-element.32.log_ref, ...), custom_call_target="tpu_custom_call" | custom-call | flops 471859200 | bytes 3744776 | tf_op jit(solution)/shard_map/pallas_call | solution.py:185
  377.7 8.3 %collective-permute-done.7.high_ref = bf16[64,1536]{1,0:T(8,128)(2,1)S(1)} collective-permute-done((bf16[64,1536]{1,0:T(8,128)(2,1)S(1)}, bf16[64,1536]{1,0:T(8,128)(2,1)S(1)}, u32[]{:S(2)}, u32[]{:S(2)}) %collective-permute-start.7) | collective-permute-done | bytes 196640 | tf_op jit(solution)/shard_map/ppermute | solution.py:413
  395.2 6.6 copy.118
  401.9 4.9 copy.119
  411.5 8.4 %copy.114 = bf16[4,768,864]{2,1,0:T(8,128)(2,1)} copy(bf16[4,768,864]{1,2,0:T(8,128)(2,1)} %pad_maximum_fusion.1) | data formatting | bytes 10616832 | tf_op jit(solution)/shard_map/concatenate | solution.py:382
  419.9 5.7 copy.115
  435.9 14.4 %pad_maximum_fusion = bf16[4,768,1632]{1,2,0:T(8,128)(2,1)} fusion(bf16[4,768,192]{1,2,0:T(8,128)(2,1)S(1)} %fusion.22, bf16[4,768,576]{1,2,0:T(8,128)(2,1)S(1)} %fusion.9, bf16[4,768,288]{1,2,0:T(8,128)(2,1)S(1)} %fusion.20, bf16[4,768,576]{1,2,0:T(8,128)(2,1)S(1)} %fusion.8), kind=kLoop, calls=%fused_computation | loop fusion | flops 40108032 | bytes 20054016 | tf_op jit(solution)/shard_map/concatenate | solution.py:423
  450.2 14.1 %copy.112 = bf16[4,768,1632]{2,1,0:T(8,128)(2,1)} copy(bf16[4,768,1632]{1,2,0:T(8,128)(2,1)} %pad_maximum_fusion) | data formatting | bytes 20054016 | tf_op jit(solution)/shard_map/concatenate | solution.py:423
  464.3 10.3 %copy.113 = bf16[8,4,96,1632]{3,2,1,0:T(8,128)(2,1)} copy(bf16[8,4,96,1632]{3,2,0,1:T(8,128)(2,1)} %bitcast.276) | data formatting | bytes 20054016 | tf_op jit(solution)/shard_map/transpose | solution.py:202
  474.8 44.9 %reduce-scatter.7.cloned.1.call-done = bf16[4,96,864]{2,1,0:T(8,128)(2,1)} async-done(((bf16[32,96,864]{2,1,0:T(8,128)(2,1)}), bf16[4,96,864]{2,1,0:T(8,128)(2,1)}) %reduce-scatter.7.cloned.1.call-update) | async-done | bytes 663568 | tf_op jit(solution)/shard_map/reduce_scatter | solution.py:204
  519.7 84.0 %reduce-scatter.5.cloned.1.call-done = bf16[4,96,1632]{2,1,0:T(8,128)(2,1)} async-done(((bf16[32,96,1632]{2,1,0:T(8,128)(2,1)}), bf16[4,96,1632]{2,1,0:T(8,128)(2,1)}) %reduce-scatter.5.cloned.1.call-update) | async-done | bytes 1253392 | tf_op jit(solution)/shard_map/reduce_scatter | solution.py:204
  603.7 5.6 concatenate.173
  635.7 25.5 %reduce-scatter.11.cloned.1.call-done = bf16[1,96,3264]{2,1,0:T(8,128)(2,1)} async-done(((bf16[4,96,3264]{2,1,0:T(8,128)(2,1)}), bf16[1,96,3264]{2,1,0:T(8,128)(2,1)}) %reduce-scatter.11.cloned.1.call-update) | async-done | bytes 626704 | tf_op jit(solution)/shard_map/reduce_scatter | solution.py:439
  (327 shorter events, 199.9 us)
Async XLA Ops:
  7.2 96.3 %all-gather.5.cloned.1.call-start = ((), (), s32[]{:S(2)}) async-start(), calls=%async_computation.8 | async-start | bytes 10543104 | tf_op jit(solution)/shard_map/all_gather | solution.py:196
  15.7 174.3 %all-gather.7.cloned.1.call-start = ((), (), s32[]{:S(2)}) async-start(), calls=%async_computation.9 | async-start | bytes 10543104 | tf_op jit(solution)/shard_map/all_gather | solution.py:196
  17.2 457.6 %reduce-scatter.9.cloned.1.call-start = ((), (), s32[]{:S(2)}) async-start(), calls=%async_computation.6 | async-start | bytes 5308416 | tf_op jit(solution)/shard_map/reduce_scatter | solution.py:204
  17.3 184.4 %copy-start.4 = (bf16[192,768]{1,0:T(8,128)(2,1)}, bf16[192,768]{1,0:T(8,128)(2,1)S(1)}, u32[]{:S(2)}) copy-start(bf16[192,768]{1,0:T(8,128)(2,1)S(1)} %convert_element_type.110) | copy-start | bytes 884740
  18.9 177.2 %copy-start.48 = (f32[192]{0:T(256)}, f32[192]{0:T(256)S(1)}, u32[]{:S(2)}) copy-start(f32[192]{0:T(256)S(1)} %broadcast_multiply_fusion.15) | copy-start | bytes 2308
  19.1 177.8 %copy-start.54 = (f32[192]{0:T(256)}, f32[192]{0:T(256)S(1)}, u32[]{:S(2)}) copy-start(f32[192]{0:T(256)S(1)} %add_rsqrt_fusion.3) | copy-start | bytes 2308
  19.3 176.8 %copy-start.10 = (bf16[192,768]{1,0:T(8,128)(2,1)}, bf16[192,768]{1,0:T(8,128)(2,1)S(1)}, u32[]{:S(2)}) copy-start(bf16[192,768]{1,0:T(8,128)(2,1)S(1)} %multiply_convert_fusion.13) | copy-start | bytes 884740
  196.9 7.8 %collective-permute-start = (bf16[64,1536]{1,0:T(8,128)(2,1)S(1)}, bf16[64,1536]{1,0:T(8,128)(2,1)S(1)}, u32[]{:S(2)}, u32[]{:S(2)}) collective-permute-start(bf16[64,1536]{1,0:T(8,128)(2,1)S(1)} %get-tuple-element.109), channel_id=1, source_target_pairs={{0,1},{1,2},{2,3},{3,4},{4,5},{5,6},{6,7},{7,8},{8,9},{9,10},{10,1... | collective-permute-start | bytes 589832 | tf_op jit(solution)/shard_map/ppermute | solution.py:31
  200.2 12.3 %collective-permute-start.1 = (bf16[64,1536]{1,0:T(8,128)(2,1)S(1)}, bf16[64,1536]{1,0:T(8,128)(2,1)S(1)}, u32[]{:S(2)}, u32[]{:S(2)}) collective-permute-start(bf16[64,1536]{1,0:T(8,128)(2,1)S(1)} %get-tuple-element.108), channel_id=1, source_target_pairs={{1,0},{2,1},{3,2},{4,3},{5,4},{6,5},{7,6},{8,7},{9,8},{10,9},{11,1... | collective-permute-start | bytes 589832 | tf_op jit(solution)/shard_map/ppermute | solution.py:33
  259.2 9.0 %collective-permute-start.2 = (bf16[64,1536]{1,0:T(8,128)(2,1)}, bf16[64,1536]{1,0:T(8,128)(2,1)S(1)}, u32[]{:S(2)}, u32[]{:S(2)}) collective-permute-start(bf16[64,1536]{1,0:T(8,128)(2,1)} %get-tuple-element.105), channel_id=1, source_target_pairs={{0,1},{1,2},{2,3},{3,4},{4,5},{5,6},{6,7},{7,8},{8,9},{9,10},{10,1... | collective-permute-start | bytes 589832 | tf_op jit(solution)/shard_map/ppermute | solution.py:31
  266.3 8.6 %collective-permute-start.3 = (bf16[64,1536]{1,0:T(8,128)(2,1)S(1)}, bf16[64,1536]{1,0:T(8,128)(2,1)S(1)}, u32[]{:S(2)}, u32[]{:S(2)}) collective-permute-start(bf16[64,1536]{1,0:T(8,128)(2,1)S(1)} %get-tuple-element.104), channel_id=1, source_target_pairs={{1,0},{2,1},{3,2},{4,3},{5,4},{6,5},{7,6},{8,7},{9,8},{10,9},{11,1... | collective-permute-start | bytes 589832 | tf_op jit(solution)/shard_map/ppermute | solution.py:33
  314.0 5.8 collective-permute-start.4
  316.3 12.7 %collective-permute-start.5 = (bf16[64,1536]{1,0:T(8,128)(2,1)S(1)}, bf16[64,1536]{1,0:T(8,128)(2,1)S(1)}, u32[]{:S(2)}, u32[]{:S(2)}) collective-permute-start(bf16[64,1536]{1,0:T(8,128)(2,1)S(1)} %get-tuple-element.112), channel_id=1, source_target_pairs={{1,0},{2,1},{3,2},{4,3},{5,4},{6,5},{7,6},{8,7},{9,8},{10,9},{11,1... | collective-permute-start | bytes 589832 | tf_op jit(solution)/shard_map/ppermute | solution.py:413
  370.9 6.8 %collective-permute-start.6 = (bf16[64,1536]{1,0:T(8,128)(2,1)S(1)}, bf16[64,1536]{1,0:T(8,128)(2,1)S(1)}, u32[]{:S(2)}, u32[]{:S(2)}) collective-permute-start(bf16[64,1536]{1,0:T(8,128)(2,1)S(1)} %get-tuple-element.111), channel_id=1, source_target_pairs={{0,1},{1,2},{2,3},{3,4},{4,5},{5,6},{6,7},{7,8},{8,9},{9,10},{10,1... | collective-permute-start | bytes 589832 | tf_op jit(solution)/shard_map/ppermute | solution.py:412
  373.3 12.7 %collective-permute-start.7 = (bf16[64,1536]{1,0:T(8,128)(2,1)S(1)}, bf16[64,1536]{1,0:T(8,128)(2,1)S(1)}, u32[]{:S(2)}, u32[]{:S(2)}) collective-permute-start(bf16[64,1536]{1,0:T(8,128)(2,1)S(1)} %get-tuple-element.110), channel_id=1, source_target_pairs={{1,0},{2,1},{3,2},{4,3},{5,4},{6,5},{7,6},{8,7},{9,8},{10,9},{11,1... | collective-permute-start | bytes 589832 | tf_op jit(solution)/shard_map/ppermute | solution.py:413
  406.9 112.8 %reduce-scatter.7.cloned.1.call-start = ((), (), s32[]{:S(2)}) async-start(), calls=%async_computation.5 | async-start | bytes 6193152 | tf_op jit(solution)/shard_map/reduce_scatter | solution.py:204
  425.6 178.2 %reduce-scatter.5.cloned.1.call-start = ((), (), s32[]{:S(2)}) async-start(), calls=%async_computation.4 | async-start | bytes 11501568 | tf_op jit(solution)/shard_map/reduce_scatter | solution.py:204
  474.7 141.7 %copy-start.34 = (bf16[192,4,288]{0,2,1:T(8,128)(2,1)S(1)}, bf16[192,4,288]{0,2,1:T(8,128)(2,1)}, u32[]{:S(2)}) copy-start(bf16[192,4,288]{0,2,1:T(8,128)(2,1)} %copy-done.33) | copy-start | bytes 1327108
  474.7 186.5 %reduce-scatter.11.cloned.1.call-start = ((), (), s32[]{:S(2)}) async-start(), calls=%async_computation.7 | async-start | bytes 3194880 | tf_op jit(solution)/shard_map/reduce_scatter | solution.py:439
  613.6 1.2 collective-permute-start.8
  614.8 5.0 collective-permute-start.9
  619.9 3.8 collective-permute-start.10
  623.6 5.0 collective-permute-start.11
  628.6 6.5 collective-permute-start.12
  (59 other events, 1249.2 us)
Sparse Core Ops, SparseCore 0:
  15.8 87.6 all-gather.4
  106.4 83.4 all-gather.6
  407.0 51.5 reduce-scatter.8
  461.9 57.7 reduce-scatter.6
  523.2 80.5 reduce-scatter.4
  609.5 51.6 reduce-scatter.10
where the time goes:
time: 681 us; the launch traced here: 673 us
  waiting for transfers between devices  363 us (53%)
  matrix products  105 us (15%)
  local copies, waits for them, and re-layouts  98.5 us (14%)
  other arithmetic  40 us (6%)
  Pallas kernels  28.6 us (4%)
  starting transfers between devices  22.2 us (3%)
  between operations  15.8 us (2%)
    all_gather x2, waiting for transfers between devices, gather_all(): whole = lax.all_gather(share, ('wshard', 'seq'), axis=0, tiled=False)  161 us
    reduce_scatter x3, waiting for transfers between devices, sum_over_blocks(): return lax.psum_scatter(parts, 'seq', scatter_dimension=0, tiled=True)  129 us
    dot_general x32, matrix products, columns_product(): jnp.dot(left, weight[i], preferred_element_type=jnp.float32)  63.5 us
    dot_general x8, matrix products, rows_product(): jnp.einsum('twf,wdf->td', left.reshape(rows, n_w, weight.shape[2]), weigh...  30.6 us
    pallas_call x8, Pallas kernels, local_call(): pl.pallas_call(kernel, out_shape=[jax.ShapeDtypeStruct(shape, kind) for s...  28.6 us
    reduce_scatter x1, waiting for transfers between devices, per_device(): lax.psum_scatter(jnp.concatenate(block_sums, axis=2), 'wshard', scatter_d...  25.5 us
    concatenate x14, local copies, waits for them, and re-layouts, columns_product(): jnp.concatenate([jnp.dot(left, weight[i], preferred_element_type=jnp.floa...  22.2 us
    transpose x3, local copies, waits for them, and re-layouts, sum_over_blocks(): terms.reshape(n_w, n_seq, depth, terms.shape[2]).transpose(1, 0, 2, 3)  21 us
  transfers between devices with their start and end apart: 19, of which 16 were waited for; matrix products, arithmetic and copies ran while one was open for 15% of the time, Pallas kernels for 0%

commit v1 on v0

--- a/solution.py
+++ b/solution.py
@@ -192,16 +192,333 @@
     )(*operands)
 
 
-def gather_all(share, n_w, n_seq):
-    whole = lax.all_gather(share, ("wshard", "seq"), axis=0, tiled=False)
-    return whole.reshape(n_w, n_seq * share.shape[0], share.shape[1])
-
-
-def sum_over_blocks(terms, n_w, n_seq):
-    depth = terms.shape[1] // n_seq
-    parts = terms.reshape(n_w, n_seq, depth, terms.shape[2]).transpose(1, 0, 2, 3)
-    parts = parts.reshape(n_seq * n_w, depth, terms.shape[2])
-    return lax.psum_scatter(parts, "seq", scatter_dimension=0, tiled=True)
+MESH = pl.DeviceIdType.MESH
+
+
+def bit_orders(n_seq):
+    bits = n_seq.bit_length() - 1
+    upper = list(range(1, bits))
+    return upper, upper[::-1]
+
+
+def bit_of(value, bit):
+    return lax.rem(value // (1 << bit), 2)
+
+
+def flipped(value, bit):
+    return value + (1 - 2 * bit_of(value, bit)) * (1 << bit)
+
+
+def greet(n_seq, n_w, me, w):
+    barrier = pltpu.get_barrier_semaphore()
+    bits = n_seq.bit_length() - 1
+    for bit in range(bits):
+        pl.semaphore_signal(
+            barrier, inc=1, device_id={"seq": flipped(me, bit)}, device_id_type=MESH
+        )
+    for j in range(1, n_w):
+        pl.semaphore_signal(
+            barrier, inc=1, device_id={"wshard": lax.rem(w + j, n_w)}, device_id_type=MESH
+        )
+    pl.semaphore_wait(barrier, bits + n_w - 1)
+
+
+def gather_kernel(n_seq, n_w, orders, *refs):
+    n = len(orders)
+    shares, wholes, stage = refs[:n], refs[n : 2 * n], refs[2 * n : 3 * n]
+    load_sem, keep_sem, zsend, zrecv, hsend, hrecv = refs[3 * n :]
+    me = lax.axis_index("seq")
+    w = lax.axis_index("wshard")
+    bits = n_seq.bit_length() - 1
+    places = [sum(bit_of(me, bit) * (1 << k) for k, bit in enumerate(order)) for order in orders]
+    loads = [pltpu.make_async_copy(shares[c], stage[c], load_sem.at[c]) for c in range(n)]
+    keeps = [pltpu.make_async_copy(stage[c], wholes[c].at[w], keep_sem.at[c]) for c in range(n)]
+    for copy in loads:
+        copy.start()
+    greet(n_seq, n_w, me, w)
+
+    def across(c, j):
+        place = places[c]
+        return pltpu.make_async_remote_copy(
+            src_ref=shares[c].at[place],
+            dst_ref=wholes[c].at[w, place],
+            send_sem=zsend.at[c, j - 1],
+            recv_sem=zrecv.at[c, j - 1],
+            device_id={"wshard": lax.rem(w + j, n_w)},
+            device_id_type=MESH,
+        )
+
+    def within(c, k, j):
+        base = places[c] // (1 << k) * (1 << k)
+        block = wholes[c].at[lax.rem(w - j + n_w, n_w), pl.ds(base, 1 << k)]
+        return pltpu.make_async_remote_copy(
+            src_ref=block,
+            dst_ref=block,
+            send_sem=hsend.at[c, k, j - 1],
+            recv_sem=hrecv.at[c, k, j - 1],
+            device_id={"seq": flipped(me, orders[c][k])},
+            device_id_type=MESH,
+        )
+
+    def arrived(c, k, j):
+        source = lax.rem(w - j + n_w, n_w)
+        if k == 0:
+            dst = wholes[c].at[source, places[c]]
+            sem = zrecv.at[c, j - 1]
+        else:
+            base = flipped(places[c], k - 1) // (1 << (k - 1)) * (1 << (k - 1))
+            dst = wholes[c].at[source, pl.ds(base, 1 << (k - 1))]
+            sem = hrecv.at[c, k - 1, j - 1]
+        pltpu.make_async_copy(dst, dst, sem).wait()
+
+    for c in range(n):
+        for j in range(1, n_w):
+            across(c, j).start()
+    for c in range(n):
+        loads[c].wait()
+        keeps[c].start()
+    for slot in range(n + bits):
+        for k in reversed(range(bits + 1)):
+            c = slot - k
+            if not 0 <= c < n:
+                continue
+            for j in range(1, n_w):
+                arrived(c, k, j)
+                if k < bits:
+                    within(c, k, j).start()
+    for c in range(n):
+        keeps[c].wait()
+        for j in range(1, n_w):
+            across(c, j).wait_send()
+            for k in range(bits):
+                within(c, k, j).wait_send()
+
+
+def gather_weights(shares, orders, n_seq, n_w):
+    n = len(shares)
+    bits = n_seq.bit_length() - 1
+    dma = pltpu.SemaphoreType.DMA
+    return pl.pallas_call(
+        lambda *refs: gather_kernel(n_seq, n_w, orders, *refs),
+        out_shape=[jax.ShapeDtypeStruct((n_w,) + s.shape, s.dtype) for s in shares],
+        in_specs=[pl.BlockSpec(memory_space=pl.ANY)] * n,
+        out_specs=[pl.BlockSpec(memory_space=pl.ANY)] * n,
+        scratch_shapes=[pltpu.VMEM(s.shape, s.dtype) for s in shares]
+        + [
+            dma((n,)),
+            dma((n,)),
+            dma((n, n_w - 1)),
+            dma((n, n_w - 1)),
+            dma((n, bits, n_w - 1)),
+            dma((n, bits, n_w - 1)),
+        ],
+        compiler_params=pltpu.CompilerParams(
+            collective_id=0, has_side_effects=True, vmem_limit_bytes=60 * 1024 * 1024
+        ),
+    )(*shares)
+
+
+def column_step(width):
+    for step in (384, 256, 128):
+        if width % step == 0:
+            return step
+    return width
+
+
+def sum_kernel(n_seq, n_w, orders, scale, *refs):
+    n = len(orders)
+    lefts, rights, outs = refs[:n], refs[n : 2 * n], refs[2 * n : 3 * n]
+    rest = refs[3 * n :]
+    bits = n_seq.bit_length() - 1
+    m = bits - 1
+    count = 1 << m
+    per = 5 + 2 * m
+    pools = [rest[c * per : (c + 1) * per] for c in range(n)]
+    load_sem, xsend, xrecv, hsend, hrecv, zsend, zrecv = rest[n * per :]
+    me = lax.axis_index("seq")
+    w = lax.axis_index("wshard")
+    peer = flipped(me, 0)
+
+    def strip_of(base, order, i):
+        code = count - 1 - i
+        for k, bit in enumerate(order):
+            if code >> (m - 1 - k) & 1:
+                base = flipped(base, bit)
+        return base
+
+    def own_loads(c):
+        lbuf, rbuf = pools[c][:2]
+        for i in range(count):
+            yield pltpu.make_async_copy(
+                lefts[c].at[strip_of(me, orders[c], i)], lbuf.at[0, i], load_sem.at[c, 0]
+            )
+        yield pltpu.make_async_copy(rights[c], rbuf.at[0], load_sem.at[c, 1])
+
+    def trades(c):
+        lbuf, rbuf = pools[c][:2]
+        to = dict(device_id={"seq": peer}, device_id_type=MESH)
+        for i in range(count):
+            yield pltpu.make_async_remote_copy(
+                src_ref=lefts[c].at[strip_of(peer, orders[c], i)],
+                dst_ref=lbuf.at[1, i],
+                send_sem=xsend.at[c, 0],
+                recv_sem=xrecv.at[c, 0],
+                **to,
+            )
+        yield pltpu.make_async_remote_copy(
+            src_ref=rights[c],
+            dst_ref=rbuf.at[1],
+            send_sem=xsend.at[c, 1],
+            recv_sem=xrecv.at[c, 1],
+            **to,
+        )
+
+    def settle(ref, sem):
+        pltpu.make_async_copy(ref, ref, sem).wait()
+
+    def halve(c, k):
+        return pltpu.make_async_remote_copy(
+            src_ref=pools[c][5 + 2 * k],
+            dst_ref=pools[c][6 + 2 * k],
+            send_sem=hsend.at[c, k],
+            recv_sem=hrecv.at[c, k],
+            device_id={"seq": flipped(me, orders[c][k])},
+            device_id_type=MESH,
+        )
+
+    def across(c, j):
+        to = lax.rem(w + j, n_w)
+        return pltpu.make_async_remote_copy(
+            src_ref=pools[c][3].at[to],
+            dst_ref=pools[c][4].at[j - 1],
+            send_sem=zsend.at[c, j - 1],
+            recv_sem=zrecv.at[c, j - 1],
+            device_id={"wshard": to},
+            device_id_type=MESH,
+        )
+
+    def compute(c):
+        lbuf, rbuf, part = pools[c][:3]
+        settle(lbuf.at[0], load_sem.at[c, 0])
+        settle(rbuf.at[0], load_sem.at[c, 1])
+        settle(lbuf.at[1], xrecv.at[c, 0])
+        settle(rbuf.at[1], xrecv.at[c, 1])
+        height, rows = lbuf.shape[2:]
+        width = rbuf.shape[2]
+        step = column_step(width)
+        half = count // 2
+        groups = [(0, count)] if height % 16 == 0 else [(i, 1) for i in range(count)]
+
+        @pl.loop(0, width // step)
+        def _(t):
+            cols = pl.ds(pl.multiple_of(t * step, step), step)
+            for start, size in groups:
+                total = None
+                for h in range(2):
+                    left = lbuf[h, start : start + size].reshape(size * height, rows)
+                    term = dot_f32(left, rbuf[h, :, cols], ((1,), (0,)))
+                    total = term if total is None else total + term
+                total = total.reshape(size, height, step)
+                for i in range(size):
+                    at = start + i
+                    if at < half:
+                        pools[c][5][at, :, cols] = total[i].astype(jnp.bfloat16)
+                    else:
+                        part[at - half, :, cols] = total[i]
+
+        halve(c, 0).start()
+
+    def reduce(c, k):
+        part = pools[c][2]
+        settle(pools[c][6 + 2 * (k - 1)], hrecv.at[c, k - 1])
+        got = pools[c][6 + 2 * (k - 1)]
+        left = count >> k
+        first = part.shape[0] - left
+        send = left // 2
+        if k < m:
+            for i in range(left):
+                value = part[first + i] + got[i].astype(jnp.float32)
+                if i < send:
+                    pools[c][5 + 2 * k][i] = value.astype(jnp.bfloat16)
+                else:
+                    part[first + i] = value
+            halve(c, k).start()
+            return
+        value = part[first] + got[0].astype(jnp.float32)
+        width = pools[c][3].shape[2]
+        for i in range(n_w):
+            pools[c][3][i] = value[:, i * width : (i + 1) * width].astype(jnp.bfloat16)
+        for j in range(1, n_w):
+            across(c, j).start()
+
+    def finish(c):
+        total = pools[c][3][w].astype(jnp.float32)
+        for j in range(1, n_w):
+            settle(pools[c][4].at[j - 1], zrecv.at[c, j - 1])
+            total = total + pools[c][4][j - 1].astype(jnp.float32)
+        outs[c][...] = total * scale
+
+    greet(n_seq, n_w, me, w)
+    for c in range(n):
+        for copy in trades(c):
+            copy.start()
+        for copy in own_loads(c):
+            copy.start()
+    lag = 2
+    for slot in range(n + lag * (m + 1)):
+        for k in reversed(range(m + 2)):
+            c = slot - lag * k
+            if not 0 <= c < n:
+                continue
+            if k == 0:
+                compute(c)
+            elif k <= m:
+                reduce(c, k)
+            else:
+                finish(c)
+    for c in range(n):
+        settle(pools[c][0].at[1], xsend.at[c, 0])
+        settle(pools[c][1].at[1], xsend.at[c, 1])
+        for k in range(m):
+            halve(c, k).wait_send()
+        for j in range(1, n_w):
+            across(c, j).wait_send()
+
+
+def sum_gradients(pairs, orders, n_seq, n_w, scale):
+    n = len(pairs)
+    m = n_seq.bit_length() - 2
+    count = 1 << m
+    lefts = [left.T.reshape(n_seq, left.shape[1] // n_seq, left.shape[0]) for left, _ in pairs]
+    rights = [right for _, right in pairs]
+    scratch = []
+    outs = []
+    for left, right in zip(lefts, rights):
+        height, rows = left.shape[1:]
+        width = right.shape[1]
+        part = width // n_w
+        scratch += [
+            pltpu.VMEM((2, count, height, rows), jnp.bfloat16),
+            pltpu.VMEM((2, rows, width), jnp.bfloat16),
+            pltpu.VMEM((count // 2, height, width), jnp.float32),
+            pltpu.VMEM((n_w, height, part), jnp.bfloat16),
+            pltpu.VMEM((n_w - 1, height, part), jnp.bfloat16),
+        ]
+        for k in range(m):
+            scratch += [pltpu.VMEM((count >> (k + 1), height, width), jnp.bfloat16)] * 2
+        outs.append(jax.ShapeDtypeStruct((height, part), jnp.float32))
+    dma = pltpu.SemaphoreType.DMA
+    scratch += [dma((n, 2))] * 3 + [dma((n, m))] * 2 + [dma((n, n_w - 1))] * 2
+    return pl.pallas_call(
+        lambda *refs: sum_kernel(n_seq, n_w, orders, scale, *refs),
+        out_shape=outs,
+        in_specs=[pl.BlockSpec(memory_space=pl.ANY)] * (2 * n),
+        out_specs=[pl.BlockSpec(memory_space=pltpu.VMEM)] * n,
+        scratch_shapes=scratch,
+        compiler_params=pltpu.CompilerParams(
+            collective_id=1, has_side_effects=True, vmem_limit_bytes=67043328
+        ),
+    )(*lefts, *rights)
 
 
 def sum_everywhere(values, axes):
@@ -241,34 +558,37 @@
     n_seq = lax.axis_size("seq")
     n_w = lax.axis_size("wshard")
     strip = D // n_seq
-    seq_index = lax.axis_index("seq")
     col_qkv = qkv_weight.shape[2]
     col_out = output_weight.shape[2]
     col_in = input_weight.shape[2]
     row_down = down_weight.shape[1]
 
-    def own_strip(weight, axis):
-        return lax.dynamic_slice_in_dim(weight, seq_index * strip, strip, axis)
-
+    order_a, order_b = [order + [0] for order in bit_orders(n_seq)]
+    shares, orders = [], []
+    for layer_number in range(LAYERS):
+        for weight, order in ((qkv_weight, order_a), (input_weight, order_b)):
+            shares.append(weight[layer_number].reshape(n_seq, strip, weight.shape[2]))
+            orders.append(order)
+        if layer_number == 0:
+            shares.append(output_weight[0].reshape(n_seq, strip, col_out))
+            orders.append(order_b)
+            shares.append(down_weight.reshape(n_seq, LAYERS * row_down // n_seq, D))
+            orders.append(order_a)
+    for layer_number in range(1, LAYERS):
+        shares.append(output_weight[layer_number].reshape(n_seq, strip, col_out))
+        orders.append(order_b)
+    wholes = gather_weights(shares, orders, n_seq, n_w)
+    full_down_all = wholes[3].reshape(n_w, LAYERS, row_down, D)
+    places = ((0, 1, 2), (4, 5, 6))
     gathered = []
     for layer_number in range(LAYERS):
-        share = jnp.concatenate(
-            [
-                own_strip(qkv_weight[layer_number], 0),
-                own_strip(input_weight[layer_number], 0),
-                own_strip(down_weight[layer_number], 1).T,
-                own_strip(output_weight[layer_number], 0),
-            ],
-            axis=1,
-        )
-        whole = gather_all(share, n_w, n_seq)
-        ends = (col_qkv, col_qkv + col_in, col_qkv + col_in + row_down)
+        at_qkv, at_in, at_out = places[layer_number]
         gathered.append(
             (
-                whole[:, :, : ends[0]],
-                whole[:, :, ends[0] : ends[1]],
-                whole[:, :, ends[1] : ends[2]],
-                whole[:, :, ends[2] :],
+                wholes[at_qkv].reshape(n_w, D, col_qkv),
+                wholes[at_in].reshape(n_w, D, col_in),
+                full_down_all[:, layer_number],
+                wholes[at_out].reshape(n_w, D, col_out),
             )
         )
 
@@ -285,17 +605,6 @@
             weight,
             preferred_element_type=jnp.float32,
         )
-
-    def blocks(left, right, width):
-        return (
-            jnp.einsum(
-                "td,twf->wdf",
-                left,
-                right.reshape(rows, n_w, width),
-                preferred_element_type=jnp.float32,
-            )
-            * scale_grad
-        ).astype(jnp.bfloat16)
 
     hidden_state = tokens
     saved_activations = []
@@ -347,9 +656,11 @@
                 gated_linear_output,
             )
         )
-        hidden_state = middle_state + rows_product(gated_linear_output, full_down)
+        hidden_state = middle_state + jnp.dot(
+            gated_linear_output, full_down.reshape(n_w * row_down, D), preferred_element_type=jnp.float32
+        )
     grad = cotangent
-    list_again, list_fgain, block_sums = ([], [], [])
+    list_again, list_fgain, grad_pairs = ([], [], [])
     for layer_number in reversed(range(LAYERS)):
         (
             holding,
@@ -368,20 +679,19 @@
         ) = saved_activations[layer_number]
         full_qkv, full_in, full_down, full_out = gathered[layer_number]
         grad_rounded = grad.astype(jnp.bfloat16)
-        local_down = blocks(grad_rounded, gated_linear_output, row_down)
-        grad_geglu = columns_product(grad_rounded, full_down)
+        grad_geglu = lax.dot_general(
+            grad_rounded,
+            full_down.reshape(n_w * row_down, D),
+            (((1,), (1,)), ((), ())),
+            preferred_element_type=jnp.float32,
+        )
         gate = inner_activation[:, :FF]
         upper = inner_activation[:, FF:]
         grad_inner = jnp.concatenate(
             [grad_geglu * upper * gelu_slope(gate), grad_geglu * gelu_exact(gate)], axis=1
         ).astype(jnp.bfloat16)
-        local_in = blocks(feedforward_normalized, grad_inner, col_in)
-        feed_terms = [local_in, local_down]
-        if layer_number == 0:
-            block_sums.append(
-                sum_over_blocks(jnp.concatenate(feed_terms, axis=2), n_w, n_seq)
-            )
-            feed_terms = []
+        grad_pairs.append((feedforward_normalized, grad_inner))
+        grad_pairs.append((grad_rounded, gated_linear_output))
         normalized_gradient = rows_product(grad_inner, full_in)
         partial_gradient, feedforward_gain_gradient = norm_backward_step(
             normalized_gradient,
@@ -392,7 +702,7 @@
         list_fgain.append(feedforward_gain_gradient * scale_grad)
         grad_middle = grad + partial_gradient
         grad_middle_rounded = grad_middle.astype(jnp.bfloat16)
-        local_out = blocks(context_rows, grad_middle_rounded, col_out)
+        grad_pairs.append((context_rows, grad_middle_rounded))
         grad_context = (
             rows_product(grad_middle_rounded, full_out).astype(jnp.bfloat16)
         )
@@ -417,12 +727,7 @@
             12 * rows * D,
             (grad_queries, local_terms, low, high, cosine, sine),
         )
-        local_qkv = blocks(attention_normalized, grad_qkv, col_qkv)
-        block_sums.append(
-            sum_over_blocks(
-                jnp.concatenate(feed_terms + [local_qkv, local_out], axis=2), n_w, n_seq
-            )
-        )
+        grad_pairs.append((attention_normalized, grad_qkv))
         attention_normalized_gradient = rows_product(grad_qkv, full_qkv)
         attention_partial_gradient, attention_gain_gradient = norm_backward_step(
             attention_normalized_gradient,
@@ -436,17 +741,12 @@
         jnp.concatenate([jnp.stack(list_again[::-1]), jnp.stack(list_fgain[::-1])], axis=0),
         ("seq", "wshard"),
     )
-    summed = lax.psum_scatter(
-        jnp.concatenate(block_sums, axis=2), "wshard", scatter_dimension=0, tiled=True
-    )[0].astype(jnp.float32)
-    per_layer = (col_in, row_down, col_qkv, col_out)
-    pieces = []
-    start = 0
-    for width in per_layer * LAYERS:
-        pieces.append(summed[:, start : start + width])
-        start += width
+    pair_orders = bit_orders(n_seq)
+    summed = sum_gradients(
+        grad_pairs, [pair_orders[(1, 0, 1, 0)[i % 4]] for i in range(len(grad_pairs))], n_seq, n_w, scale_grad
+    )
     by_kind = [
-        jnp.stack([pieces[4 * (LAYERS - 1 - n) + kind] for n in range(LAYERS)]) for kind in range(4)
+        jnp.stack([summed[4 * (LAYERS - 1 - n) + kind] for n in range(LAYERS)]) for kind in (0, 1, 3, 2)
     ]
     return (
         hidden_state,

time: 681 us -> 456 us (0.67)
  waiting for transfers between devices: 363 us -> 21.1 us
  Pallas kernels: 28.6 us -> 269 us
  matrix products: 105 us -> 38.8 us
  local copies, waits for them, and re-layouts: 98.5 us -> 60.2 us
  other arithmetic: 40 us -> 22.8 us
  between operations: 15.8 us -> 2.27 us
  starting transfers between devices: 22.2 us -> 35.3 us
    pallas_call x0 -> x2, Pallas kernels: none -> 241 us  [the longest x1 124 us: sum_gradients(): pl.pallas_call(lambda *refs: sum_kernel(n_seq, n_w, orders, scale, *refs)...]
    all_gather x2 -> x0, waiting for transfers between devices: 161 us -> none  [gather_all(): whole = lax.all_gather(share, ('wshard', 'seq'), axis=0, tiled=False)]
    reduce_scatter x4 -> x0, waiting for transfers between devices: 154 us -> none  [the longest x3 129 us: sum_over_blocks(): return lax.psum_scatter(parts, 'seq', scatter_dimension=0, tiled=True)]
    dot_general x32 -> x24, matrix products: 63.5 us -> 13.9 us  [columns_product(): jnp.dot(left, weight[i], preferred_element_type=jnp.float32)]
    concatenate x6 -> x8, local copies, waits for them, and re-layouts: 36.5 us -> 3.14 us  [per_device(): jnp.concatenate([grad_geglu * upper * gelu_slope(gate), grad_geglu * gelu...]
    slice x4 -> x13, local copies, waits for them, and re-layouts: 5.36 us -> 26 us  [the longest x3 11.5 us: columns_product(): weight[i]]
    concatenate x14 -> x2, local copies, waits for them, and re-layouts: 22.2 us -> 3.52 us  [columns_product(): jnp.concatenate([jnp.dot(left, weight[i], preferred_element_type=jnp.floa...]
    transpose x3, local copies, waits for them, and re-layouts: 21 us -> 3.72 us  [sum_gradients(): left.T.reshape(n_seq, left.shape[1] // n_seq, left.shape[0])]
  transfers between devices with their start and end apart: 19 -> 13, of which waited for: 16 -> 7; matrix products, arithmetic and copies ran while one was open for 15% -> 8% of each run, Pallas kernels for 0% -> 28%
where the time goes in v1:
time: 456 us; the launch traced here: 450 us
  Pallas kernels  269 us (59%)
  local copies, waits for them, and re-layouts  60.2 us (13%)
  matrix products  38.8 us (9%)
  starting transfers between devices  35.3 us (8%)
  other arithmetic  22.8 us (5%)
  waiting for transfers between devices  21.1 us (5%)
    pallas_call x1, Pallas kernels, sum_gradients(): pl.pallas_call(lambda *refs: sum_kernel(n_seq, n_w, orders, scale, *refs)...  124 us
    pallas_call x1, Pallas kernels, gather_weights(): pl.pallas_call(lambda *refs: gather_kernel(n_seq, n_w, orders, *refs), ou...  117 us
    pallas_call x8, Pallas kernels, local_call(): pl.pallas_call(kernel, out_shape=[jax.ShapeDtypeStruct(shape, kind) for s...  28.3 us
    dot_general x6, matrix products, rows_product(): jnp.einsum('twf,wdf->td', left.reshape(rows, n_w, weight.shape[2]), weigh...  18.5 us
    ppermute x2, starting transfers between devices, with_halo(): lax.ppermute(tail, axis, [(i, (i + 1) % count) for i in range(ends)])  17.2 us
    dot_general x24, matrix products, columns_product(): jnp.dot(left, weight[i], preferred_element_type=jnp.float32)  13.9 us
    slice x3, local copies, waits for them, and re-layouts, columns_product(): weight[i]  11.5 us
    ppermute x2, waiting for transfers between devices, per_device(): lax.ppermute(rims[:WIN], sites, [(i + 1, i) for i in range(count - 1)])  10.2 us
  transfers between devices with their start and end apart: 13, of which 7 were waited for; matrix products, arithmetic and copies ran while one was open for 8% of the time, Pallas kernels for 28%

profile of v1, /device:TPU:0, one launch (start us, length us, event | category | flops | bytes accessed | tf_op | source)
XLA Modules:
  0.0 449.9 jit_solution(7276561760658032370)
XLA Ops:
  11.4 116.8 %shard_map.143 = (bf16[4,8,96,576]{3,2,1,0:T(8,128)(2,1)}, bf16[4,8,96,576]{3,2,1,0:T(8,128)(2,1)}, bf16[4,8,96,192]{3,2,1,0:T(8,128)(2,1)}, bf16[4,8,72,768]{3,...) custom-call(bf16[8,96,576]{2,1,0:T(8,128)(2,1)} %bitcast.160, ...), custom_call_target="tpu_custom_call" | custom-call | tf_op jit(solution)/shard_map/pallas_call | solution.py:301
  128.2 5.0 %fusion.37 = (bf16[1,8,96,576]{3,2,1,0:T(8,128)(2,1)}, bf16[1,8,96,576]{3,2,1,0:T(8,128)(2,1)}, bf16[1,8,96,576]{3,2,1,0:T(8,128)(2,1)}, bf16[1,8,96,576]{3,2,1,...) fusion(bf16[4,8,96,576]{3,2,1,0:T(8,128)(2,1)} %get-tuple-eleme, ...), kind=kLoop, calls=%fused_computation.136 | loop fusion | bytes 14155776 | tf_op jit(solution)/shard_map/slice | solution.py:597
  141.4 12.5 %collective-permute-start = (bf16[64,1536]{1,0:T(8,128)(2,1)}, bf16[64,1536]{1,0:T(8,128)(2,1)}, u32[]{:S(2)}, u32[]{:S(2)}) collective-permute-start(bf16[64,1536]{1,0:T(8,128)(2,1)} %get-tuple-element.139), channel_id=1, source_target_pairs={{0,1},{1,2},{2,3},{3,4},{4,5},{5,6},{6,7},{7,8},{8,9},{9,10},{10,1... | collective-permute-start | bytes 589832 | tf_op jit(solution)/shard_map/ppermute | solution.py:31
  156.3 4.2 fusion.39
  162.4 2.8 fusion.42
  165.2 3.7 fusion.35
  170.6 5.8 %shard_map.145 = (bf16[192,768]{1,0:T(8,128)(2,1)S(1)}, f32[192,12]{1,0:T(8,128)S(1)}) custom-call(s32[2]{0:T(128)S(1)} %pad_add_fusion.bounds_ref, bf16[192,768]{1,0:T(8,128)(2,1)S(1)} %get-tuple-element.38.query_ref, bf16[320,1536]{1,0:T(8,128)(2,1)S(1)} %constant_dynamic-update-slice_fusion.kv_ref), custom_call_target="tpu_custom_call" | custom-call | flops 188743680 | bytes 1582088 | tf_op jit(solution)/shard_map/pallas_call | solution.py:185
  191.2 4.7 %collective-permute-start.2 = (bf16[64,1536]{1,0:T(8,128)(2,1)S(1)}, bf16[64,1536]{1,0:T(8,128)(2,1)S(1)}, u32[]{:S(2)}, u32[]{:S(2)}) collective-permute-start(bf16[64,1536]{1,0:T(8,128)(2,1)S(1)} %get-tuple-element.137), channel_id=1, source_target_pairs={{0,1},{1,2},{2,3},{3,4},{4,5},{5,6},{6,7},{7,8},{8,9},{9,10},{10,1... | collective-permute-start | bytes 589832 | tf_op jit(solution)/shard_map/ppermute | solution.py:31
  201.3 5.6 %collective-permute-done.3 = bf16[64,1536]{1,0:T(8,128)(2,1)S(1)} collective-permute-done((bf16[64,1536]{1,0:T(8,128)(2,1)S(1)}, bf16[64,1536]{1,0:T(8,128)(2,1)S(1)}, u32[]{:S(2)}, u32[]{:S(2)}) %collective-permute-start.3) | collective-permute-done | bytes 196640 | tf_op jit(solution)/shard_map/ppermute | solution.py:33
  206.9 5.8 %shard_map.147 = (bf16[192,768]{1,0:T(8,128)(2,1)S(1)}, f32[192,12]{1,0:T(8,128)S(1)}) custom-call(s32[2]{0:T(128)S(1)} %pad_add_fusion.bounds_ref, bf16[192,768]{1,0:T(8,128)(2,1)S(1)} %get-tuple-element.45.query_ref, bf16[320,1536]{1,0:T(8,128)(2,1)S(1)} %constant_dynamic-update-slice_fusion.3.kv_ref), custom_call_target="tpu_custom_call" | custom-call | flops 188743680 | bytes 1582088 | tf_op jit(solution)/shard_map/pallas_call | solution.py:185
  222.1 2.3 pad_maximum_fusion.4.refs_8_
  232.1 6.6 %shard_map.148 = (f32[192,768]{1,0:T(8,128)S(1)}, f32[192,1536]{1,0:T(8,128)S(1)}, bf16[128,1536]{1,0:T(8,128)(2,1)S(1)}) custom-call(s32[2]{0:T(128)S(1)} %pad_add_fusion.bounds_ref, bf16[192,768]{1,0:T(8,128)(2,1)S(1)} %copy-done.7, bf16[320,1536]{1,0:T(8,128)(2,1)S(1)} %constant_dynamic-update-slice_fusion.3.kv_ref, ...), custom_call_target="tpu_custom_call" | custom-call | flops 471859200 | bytes 3744776 | tf_op jit(solution)/shard_map/pallas_call | solution.py:185
  239.4 2.4 collective-permute-start.4
  249.2 3.0 convolution_add_fusion
  252.2 2.4 collective-permute-done.5.high_ref
  257.6 4.7 %multiply_reduce_fusion.2 = (f32[768]{0:T(1024)}, f32[192]{0:T(256)S(1)}, f32[192]{0:T(256)S(1)}, f32[192,768]{1,0:T(8,128)S(1)}) fusion(f32[192,768]{1,0:T(8,128)S(1)} %copy-done.17, f32[192]{0:T(256)S(1)} %copy-done.77, f32[192]{0:T(256)S(1)} %copy-done.71, f32[768]{0:T(1024)S(1)} %get-tuple-element.88, bf16[4,768,576]{2,1,0:T(8,128)(2,1)} %bitcast.166, ...), kind=kOutput, calls=%fused_computation.51 | convolution fusion | flops 680655744 | bytes 5612544 | tf_op jit(solution)/shard_map/twf,wdf->td/dot_general | solution.py:602
  266.3 3.7 multiply_reduce_fusion.1
  274.6 6.7 %shard_map.150 = (f32[192,768]{1,0:T(8,128)S(1)}, f32[192,1536]{1,0:T(8,128)S(1)}, bf16[128,1536]{1,0:T(8,128)(2,1)S(1)}) custom-call(s32[2]{0:T(128)S(1)} %pad_add_fusion.bounds_ref, bf16[192,768]{1,0:T(8,128)(2,1)S(1)} %copy-done.5, bf16[320,1536]{1,0:T(8,128)(2,1)S(1)} %copy-done.3, f32[192,12]{1,0:T(8,128)S(1)} %get-tuple-element.54.log_ref, ...), custom_call_target="tpu_custom_call" | custom-call | flops 471859200 | bytes 3744776 | tf_op jit(solution)/shard_map/pallas_call | solution.py:185
  281.3 2.9 collective-permute-start.6
  289.6 7.8 %collective-permute-done.7.high_ref = bf16[64,1536]{1,0:T(8,128)(2,1)S(1)} collective-permute-done((bf16[64,1536]{1,0:T(8,128)(2,1)S(1)}, bf16[64,1536]{1,0:T(8,128)(2,1)S(1)}, u32[]{:S(2)}, u32[]{:S(2)}) %collective-permute-start.7) | collective-permute-done | bytes 196640 | tf_op jit(solution)/shard_map/ppermute | solution.py:723
  299.7 3.8 multiply_reduce_fusion.3
  305.3 124.3 %shard_map.152 = (f32[96,576]{1,0:T(8,128)}, f32[96,288]{1,0:T(8,128)}, f32[96,192]{1,0:T(8,128)}, f32[96,576]{1,0:T(8,128)}, f32[96,576]{1,0:T(8,128)}, /*index...) custom-call(bf16[8,96,192]{2,1,0:T(8,128)(2,1)} %bitcast.189, bf16[8,96,192]{2,1,0:T(8,128)(2,1)} %bitcast.190, ...), custom_call_target="tpu_custom_call" | custom-call | tf_op jit(solution)/shard_map/pallas_call | solution.py:512
  438.8 3.5 collective-permute-start.11
  443.9 3.5 collective-permute-start.12
  (318 shorter events, 103.3 us)
Async XLA Ops:
  11.1 144.3 %copy-start.66 = (f32[192]{0:T(256)}, f32[192]{0:T(256)S(1)}, u32[]{:S(2)}) copy-start(f32[192]{0:T(256)S(1)} %broadcast_multiply_fusion.15) | copy-start | bytes 2308
  11.3 144.1 %copy-start.72 = (f32[192]{0:T(256)}, f32[192]{0:T(256)S(1)}, u32[]{:S(2)}) copy-start(f32[192]{0:T(256)S(1)} %add_rsqrt_fusion.3) | copy-start | bytes 2308
  140.6 30.0 %copy-start.4 = (bf16[192,768]{1,0:T(8,128)(2,1)}, bf16[192,768]{1,0:T(8,128)(2,1)S(1)}, u32[]{:S(2)}) copy-start(bf16[192,768]{1,0:T(8,128)(2,1)S(1)} %get-tuple-element.38.query_ref) | copy-start | bytes 884740
  141.4 28.1 %collective-permute-start = (bf16[64,1536]{1,0:T(8,128)(2,1)}, bf16[64,1536]{1,0:T(8,128)(2,1)}, u32[]{:S(2)}, u32[]{:S(2)}) collective-permute-start(bf16[64,1536]{1,0:T(8,128)(2,1)} %get-tuple-element.139), channel_id=1, source_target_pairs={{0,1},{1,2},{2,3},{3,4},{4,5},{5,6},{6,7},{7,8},{8,9},{9,10},{10,1... | collective-permute-start | bytes 589832 | tf_op jit(solution)/shard_map/ppermute | solution.py:31
  153.9 16.7 %collective-permute-start.1 = (bf16[64,1536]{1,0:T(8,128)(2,1)}, bf16[64,1536]{1,0:T(8,128)(2,1)S(1)}, u32[]{:S(2)}, u32[]{:S(2)}) collective-permute-start(bf16[64,1536]{1,0:T(8,128)(2,1)} %get-tuple-element.138), channel_id=1, source_target_pairs={{1,0},{2,1},{3,2},{4,3},{5,4},{6,5},{7,6},{8,7},{9,8},{10,9},{11,1... | collective-permute-start | bytes 589832 | tf_op jit(solution)/shard_map/ppermute | solution.py:33
  191.2 15.7 %copy-start.6 = (bf16[192,768]{1,0:T(8,128)(2,1)}, bf16[192,768]{1,0:T(8,128)(2,1)S(1)}, u32[]{:S(2)}) copy-start(bf16[192,768]{1,0:T(8,128)(2,1)S(1)} %get-tuple-element.45.query_ref) | copy-start | bytes 884740
  191.2 10.0 %collective-permute-start.2 = (bf16[64,1536]{1,0:T(8,128)(2,1)S(1)}, bf16[64,1536]{1,0:T(8,128)(2,1)S(1)}, u32[]{:S(2)}, u32[]{:S(2)}) collective-permute-start(bf16[64,1536]{1,0:T(8,128)(2,1)S(1)} %get-tuple-element.137), channel_id=1, source_target_pairs={{0,1},{1,2},{2,3},{3,4},{4,5},{5,6},{6,7},{7,8},{8,9},{9,10},{10,1... | collective-permute-start | bytes 589832 | tf_op jit(solution)/shard_map/ppermute | solution.py:31
  195.9 11.0 %collective-permute-start.3 = (bf16[64,1536]{1,0:T(8,128)(2,1)S(1)}, bf16[64,1536]{1,0:T(8,128)(2,1)S(1)}, u32[]{:S(2)}, u32[]{:S(2)}) collective-permute-start(bf16[64,1536]{1,0:T(8,128)(2,1)S(1)} %get-tuple-element.136), channel_id=1, source_target_pairs={{1,0},{2,1},{3,2},{4,3},{5,4},{6,5},{7,6},{8,7},{9,8},{10,9},{11,1... | collective-permute-start | bytes 589832 | tf_op jit(solution)/shard_map/ppermute | solution.py:33
  214.1 13.4 %copy-start.8 = (f32[192,768]{1,0:T(8,128)}, f32[192,768]{1,0:T(8,128)S(1)}, u32[]{:S(2)}) copy-start(f32[192,768]{1,0:T(8,128)S(1)} %get-tuple-element.97) | copy-start | bytes 1769476
  239.4 12.7 %collective-permute-start.4 = (bf16[64,1536]{1,0:T(8,128)(2,1)}, bf16[64,1536]{1,0:T(8,128)(2,1)S(1)}, u32[]{:S(2)}, u32[]{:S(2)}) collective-permute-start(bf16[64,1536]{1,0:T(8,128)(2,1)} %get-tuple-element.145), channel_id=1, source_target_pairs={{0,1},{1,2},{2,3},{3,4},{4,5},{5,6},{6,7},{7,8},{8,9},{9,10},{10,1... | collective-permute-start | bytes 589832 | tf_op jit(solution)/shard_map/ppermute | solution.py:722
  241.9 12.6 %collective-permute-start.5 = (bf16[64,1536]{1,0:T(8,128)(2,1)S(1)}, bf16[64,1536]{1,0:T(8,128)(2,1)S(1)}, u32[]{:S(2)}, u32[]{:S(2)}) collective-permute-start(bf16[64,1536]{1,0:T(8,128)(2,1)S(1)} %get-tuple-element.144), channel_id=1, source_target_pairs={{1,0},{2,1},{3,2},{4,3},{5,4},{6,5},{7,6},{8,7},{9,8},{10,9},{11,1... | collective-permute-start | bytes 589832 | tf_op jit(solution)/shard_map/ppermute | solution.py:723
  274.6 12.8 %copy-start.80 = (f32[768]{0:T(1024)S(1)}, f32[768]{0:T(1024)}, u32[]{:S(2)}) copy-start(f32[768]{0:T(1024)} %get-tuple-element.76) | copy-start | bytes 9220
  281.3 8.3 %collective-permute-start.6 = (bf16[64,1536]{1,0:T(8,128)(2,1)S(1)}, bf16[64,1536]{1,0:T(8,128)(2,1)S(1)}, u32[]{:S(2)}, u32[]{:S(2)}) collective-permute-start(bf16[64,1536]{1,0:T(8,128)(2,1)S(1)} %get-tuple-element.143), channel_id=1, source_target_pairs={{0,1},{1,2},{2,3},{3,4},{4,5},{5,6},{6,7},{7,8},{8,9},{9,10},{10,1... | collective-permute-start | bytes 589832 | tf_op jit(solution)/shard_map/ppermute | solution.py:722
  284.2 13.2 %collective-permute-start.7 = (bf16[64,1536]{1,0:T(8,128)(2,1)S(1)}, bf16[64,1536]{1,0:T(8,128)(2,1)S(1)}, u32[]{:S(2)}, u32[]{:S(2)}) collective-permute-start(bf16[64,1536]{1,0:T(8,128)(2,1)S(1)} %get-tuple-element.142), channel_id=1, source_target_pairs={{1,0},{2,1},{3,2},{4,3},{5,4},{6,5},{7,6},{8,7},{9,8},{10,9},{11,1... | collective-permute-start | bytes 589832 | tf_op jit(solution)/shard_map/ppermute | solution.py:723
  287.4 16.1 %copy-start.63 = (f32[1,768]{1,0:T(1,128)}, f32[1,768]{1,0:T(1,128)S(1)}, u32[]{:S(2)}) copy-start(f32[1,768]{1,0:T(1,128)S(1)} %mul.433) | copy-start | bytes 9220
  287.4 16.1 %copy-start.64 = (f32[1,768]{1,0:T(1,128)}, f32[1,768]{1,0:T(1,128)S(1)}, u32[]{:S(2)}) copy-start(f32[1,768]{1,0:T(1,128)S(1)} %mul.430) | copy-start | bytes 9220
  304.2 125.4 %collective-permute-start.8 = (f32[4,768]{1,0:T(4,128)}, f32[4,768]{1,0:T(4,128)}, u32[]{:S(2)}, u32[]{:S(2)}) collective-permute-start(f32[4,768]{1,0:T(4,128)} %pad_maximum_fusion.11), channel_id=1, source_target_pairs={{0,4},{4,0},{8,12},{12,8},{16,20},{20,16},{24,28},{28,24},{1,5},{5... | collective-permute-start | bytes 36872 | tf_op jit(solution)/shard_map/ppermute | solution.py:533
  429.6 12.7 %copy-start.57 = (f32[96,288]{1,0:T(8,128)S(1)}, f32[96,288]{1,0:T(8,128)}, u32[]{:S(2)}) copy-start(f32[96,288]{1,0:T(8,128)} %get-tuple-element.65) | copy-start | bytes 331780
  429.6 17.9 %copy-start.59 = (f32[96,192]{1,0:T(8,128)S(1)}, f32[96,192]{1,0:T(8,128)}, u32[]{:S(2)}) copy-start(f32[96,192]{1,0:T(8,128)} %get-tuple-element.61) | copy-start | bytes 221188
  429.6 17.8 %copy-start.60 = (f32[96,192]{1,0:T(8,128)S(1)}, f32[96,192]{1,0:T(8,128)}, u32[]{:S(2)}) copy-start(f32[96,192]{1,0:T(8,128)} %get-tuple-element.60) | copy-start | bytes 221188
  430.5 3.8 collective-permute-start.9
  435.0 3.8 collective-permute-start.10
  438.8 5.1 %collective-permute-start.11 = (f32[4,768]{1,0:T(4,128)S(1)}, f32[4,768]{1,0:T(4,128)S(1)}, u32[]{:S(2)}, u32[]{:S(2)}) collective-permute-start(f32[4,768]{1,0:T(4,128)S(1)} %add.146), channel_id=1, source_target_pairs={{0,1},{1,0},{2,3},{3,2},{4,5},{5,4},{6,7},{7,6},{8,9},{9,8},{10,11... | collective-permute-start | bytes 36872 | tf_op jit(solution)/shard_map/ppermute | solution.py:533
  443.9 5.2 %collective-permute-start.12 = (f32[4,768]{1,0:T(4,128)S(1)}, f32[4,768]{1,0:T(4,128)S(1)}, u32[]{:S(2)}, u32[]{:S(2)}) collective-permute-start(f32[4,768]{1,0:T(4,128)S(1)} %add.147), channel_id=1, source_target_pairs={{0,2},{1,3},{2,0},{3,1},{4,6},{5,7},{6,4},{7,5},{8,10},{9,11},{10,... | collective-permute-start | bytes 36872 | tf_op jit(solution)/shard_map/ppermute | solution.py:533
  (70 other events, 232.4 us)
